TPU v7x, 32 devices: a whole 2x2x4 slice. The times are simulated.
32 devices in a mesh: fiber: 2 (over x), blk: 16 (over z, y, core).
Axes of the slice: x: 2, y: 2, z: 4, core: 2. Of those that a mesh axis runs over, the one named last changes fastest.
Arguments:
- users: bfloat16 [32768, 256], P('blk', 'fiber'), may hold values from -1.5 to 1.5
- items: bfloat16 [4096, 256], P('blk'), may hold values from -1.5 to 1.5
- tile_users: int32 [16, 2, 128], P('blk', 'fiber'), may hold values from 0 to 15
- tile_items: int32 [16, 2, 128], P('blk', 'fiber'), may hold values from 0 to 31, as said below
- confidence: bfloat16 [16, 2, 128, 128, 128], P('blk', 'fiber'), may hold values from 0.19921875 to 5
Outputs:
- user_grad: bfloat16 [32768, 256], P('blk', 'fiber')
Inputs may be any that keep to these rules, and one draw needn't show every extreme that they name: `tile_items`: each device's list is sorted by item block, then user block, and holds distinct pairs; the two lists of the same index of blk share no pair. A device has at most 8 tiles in any item block, and exactly 8 in at least one.
All inputs are finite; a program needn't handle non-finite values.
Results may differ from a plain program's by a relative error of at most 0.0034.
Values may be sent and summed in bfloat16 or wider, within the bound.
No kernel may reach another device: no remote copies, remote signals or barrier semaphores. Data moves between devices by JAX's collectives and lax.ppermute only.
A program may use at most 128 MiB of HBM per device.

v0:
```python
import math
import jax
import jax.numpy as jnp
from jax import lax
from jax.sharding import PartitionSpec as P


def shards(users, items, tile_users, tile_items, confidence):
    panel_rows = lax.all_gather(users, "fiber", axis=1, tiled=True)
    tile_size = confidence.shape[-1]
    rank_width = panel_rows.shape[1]
    user_count = panel_rows.shape[0] // tile_size
    panel_blocks = panel_rows.reshape(user_count, tile_size, rank_width)
    user_list = tile_users.reshape(-1)
    item_list = tile_items.reshape(-1)
    conf_tiles = confidence.reshape(-1, tile_size, tile_size)
    tile_count = user_list.shape[0]
    item_count = items.shape[0] // tile_size * lax.axis_size("blk")
    block_ids = jnp.arange(user_count, dtype=jnp.int32)

    def accumulate(totals, user_ids, conf_part, item_rows, live_mask):
        user_rows = panel_blocks[user_ids]
        scores = jnp.einsum(
            "tar,tbr->tab", user_rows, item_rows, preferred_element_type=jnp.float32
        )
        weight = (conf_part.astype(jnp.float32) * (1.0 - scores) * live_mask[:, None, None]).astype(
            jnp.bfloat16
        )
        products = jnp.einsum("tab,tbr->tar", weight, item_rows, preferred_element_type=jnp.float32)
        return totals.at[user_ids].add(products)

    empty = jnp.zeros((user_count, tile_size, rank_width), jnp.float32)
    gathered = lax.all_gather(items, "blk", axis=0, tiled=True).reshape(
        item_count, tile_size, rank_width
    )
    group = math.gcd(tile_count, 128)
    every_live = jnp.ones((group,), jnp.float32)

    def one_group(index, running):
        first = (index * group).astype(jnp.int32)
        user_ids = lax.dynamic_slice_in_dim(user_list, first, group, 0)
        item_ids = lax.dynamic_slice_in_dim(item_list, first, group, 0)
        conf_part = lax.dynamic_slice_in_dim(conf_tiles, first, group, 0)
        return accumulate(running, user_ids, conf_part, gathered[item_ids], every_live)

    totals = lax.fori_loop(0, tile_count // group, one_group, empty)
    row_sums = jnp.sum(conf_tiles, axis=-1, dtype=jnp.float32)
    owners = (user_list[:, None] == block_ids[None, :]).astype(jnp.float32)
    row_local = jnp.einsum("tk,ta->ka", owners, row_sums, precision=lax.Precision.HIGHEST).reshape(
        -1
    )
    fiber_count = lax.axis_size("fiber")
    widened = jnp.broadcast_to(row_local[:, None], (row_local.shape[0], fiber_count))
    shares, row_total = (
        lax.psum_scatter(totals.reshape(-1, rank_width), "fiber", scatter_dimension=1, tiled=True),
        lax.psum_scatter(widened, "fiber", scatter_dimension=1, tiled=True),
    )
    return (shares * lax.rsqrt(1.0 + row_total)).astype(jnp.bfloat16)


def solution(mesh):
    in_specs = (
        P("blk", "fiber"),
        P("blk", None),
        P("blk", "fiber", None),
        P("blk", "fiber", None),
        P("blk", "fiber", None, None, None),
    )
    out_specs = P("blk", "fiber")
    return jax.shard_map(shards, mesh=mesh, in_specs=in_specs, out_specs=out_specs, check_vma=False)
```

profile of v0, /device:TPU:0, one launch (start us, length us, event | category | flops | bytes accessed | tf_op | source)
XLA Modules:
  0.0 168.0 jit_solution(1765805471388297682)
XLA Ops:
  6.5 0.0 all-gather.3.cloned.1.call-start
  6.5 0.7 all-gather.3.cloned.1.call-update
  7.3 0.0 all-gather.5.cloned.1.call-start
  7.3 0.7 all-gather.5.cloned.1.call-update
  8.0 0.0 reduce-scatter.2.cloned.1.call-start
  8.1 0.7 fusion.9
  8.7 0.7 fusion.10
  9.4 23.5 %all-gather.3.cloned.1.call-done = bf16[2048,256]{1,0:T(8,128)(2,1)} async-done(((bf16[2048,128]{1,0:T(8,128)(2,1)}), bf16[2048,256]{1,0:T(8,128)(2,1)}) %all-gather.3.cloned.1.call-update) | async-done | bytes 1048592 | tf_op jit(solution)/shard_map/all_gather | solution.py:9
  32.9 7.7 %gather_fusion = bf16[128,128,256]{2,1,0:T(8,128)(2,1)} fusion(bf16[16,128,256]{2,1,0:T(8,128)(2,1)} %bitcast.28, s32[1024]{0:T(1024)S(1)} %pad_clamp_fusion.1), kind=kCustom, calls=%fused_computation | custom fusion | bytes 16777728 | tf_op jit(solution)/shard_map/while/body/eval_jaxpr/gather | solution.py:22
  40.6 35.9 %all-gather.5.cloned.1.call-done = bf16[4096,256]{1,0:T(8,128)(2,1)} async-done(((bf16[256,256]{1,0:T(8,128)(2,1)}), bf16[4096,256]{1,0:T(8,128)(2,1)}) %all-gather.5.cloned.1.call-update) | async-done | bytes 2097168 | tf_op jit(solution)/shard_map/all_gather | solution.py:33
  76.5 8.1 %gather_fusion.1 = bf16[128,128,256]{2,1,0:T(8,128)(2,1)} fusion(bf16[32,128,256]{2,1,0:T(8,128)(2,1)} %bitcast.29, s32[1024]{0:T(1024)S(1)} %pad_clamp_fusion), kind=kCustom, calls=%fused_computation.1 | custom fusion | bytes 16777728 | tf_op jit(solution)/shard_map/while/body/eval_jaxpr/gather | solution.py:44
  84.7 17.4 %fusion.2 = f32[128,128,256]{2,1,0:T(8,128)} fusion(bf16[128,128,256]{2,1,0:T(8,128)(2,1)} %gather_fusion.1, bf16[1,1,128,128,128]{4,3,2,1,0:T(8,128)(2,1)} %param.9, bf16[128,128,256]{2,1,0:T(8,128)(2,1)} %gather_fusion), kind=kOutput, calls=%fused_computation.7 | convolution fusion | flops 2155872256 | bytes 37748736 | tf_op jit(solution)/shard_map/while/body/eval_jaxpr/tab,tbr->tar/dot_general | solution.py:29
  102.1 0.2 broadcast_in_dim.16
  102.3 0.0 copy-start.2
  102.3 0.0 copy-start.1
  102.3 24.4 %scatter_fusion = f32[16,128,256]{2,1,0:T(8,128)S(1)} fusion(f32[16,128,256]{2,1,0:T(8,128)S(1)} %broadcast_in_dim.16, s32[128]{0:T(128)S(1)} %fusion.9, f32[128,128,256]{2,1,0:T(8,128)} %fusion.2), kind=kCustom, calls=%fused_computation.2 | custom fusion | flops 4194304 | bytes 50332160 | tf_op jit(solution)/shard_map/while/body/eval_jaxpr/scatter-add | solution.py:30
  126.6 0.0 copy-start
  126.7 1.3 copy-done
  128.0 0.0 reduce-scatter.2.cloned.1.call-update
  128.0 0.0 copy-done.2
  128.0 0.6 dynamic-slice
  128.6 3.4 %convert_reduce_fusion = f32[128,128]{1,0:T(8,128)S(1)} fusion(bf16[1,1,128,128,128]{4,3,2,1,0:T(8,128)(2,1)} %param.9), kind=kLoop, calls=%fused_computation.3 | loop fusion | flops 4177920 | bytes 4259840 | tf_op jit(solution)/shard_map/reduce_sum | solution.py:47
  132.0 0.0 copy-done.1
  132.0 0.3 convolution_bitcast_fusion
  132.3 8.7 %all-reduce = f32[2048,2]{0,1:T(2,128)S(1)} all-reduce(f32[2048,2]{0,1:T(2,128)S(1)} %broadcast_in_dim.18), channel_id=3, replica_groups=mesh['fiber'=2,'blk'=16] {'fiber'}, use_global_device_ids=true, to_apply=%region_3.0.clone | all-reduce | flops 4096 | bytes 32768
  141.0 0.7 fusion.8
  141.7 17.5 %reduce-scatter.2.cloned.1.call-done = f32[2048,128]{1,0:T(8,128)} async-done(((f32[2048,256]{1,0:T(8,128)}), f32[2048,128]{1,0:T(8,128)}) %reduce-scatter.2.cloned.1.call-update) | async-done | bytes 1048592 | tf_op jit(solution)/shard_map/reduce_scatter | solution.py:55
  159.1 2.4 %multiply_convert_fusion = bf16[2048,128]{1,0:T(8,128)(2,1)} fusion(f32[2048,128]{1,0:T(8,128)} %reduce-scatter.2.cloned.1.call-done, f32[2048]{0:T(1024)S(1)} %bitcast.30), kind=kLoop, calls=%fused_computation.11 | loop fusion | flops 524288 | bytes 1581056 | tf_op jit(solution)/shard_map/convert_element_type | solution.py:58
  (3 shorter events, 0.0 us)
Async XLA Ops:
  6.5 26.3 %all-gather.3.cloned.1.call-start = ((), (), s32[]{:S(2)}) async-start(), calls=%async_computation.1 | async-start | bytes 1572864 | tf_op jit(solution)/shard_map/all_gather | solution.py:9
  7.3 69.3 %all-gather.5.cloned.1.call-start = ((), (), s32[]{:S(2)}) async-start(), calls=%async_computation.2 | async-start | bytes 2228224 | tf_op jit(solution)/shard_map/all_gather | solution.py:33
  8.0 151.1 %reduce-scatter.2.cloned.1.call-start = ((), (), s32[]{:S(2)}) async-start(), calls=%async_computation.3 | async-start | bytes 3145728 | tf_op jit(solution)/shard_map/reduce_scatter | solution.py:55
  102.3 25.8 %copy-start.2 = (u32[32]{0:T(128)S(1)}, u32[32]{0:T(128)}, u32[]{:S(2)}) copy-start(u32[32]{0:T(128)} %constant.29) | copy-start | bytes 388
  102.3 29.7 %copy-start.1 = (s32[1,1,128]{2,1,0:T(1,128)S(1)}, s32[1,1,128]{2,1,0:T(1,128)}, u32[]{:S(2)}) copy-start(s32[1,1,128]{2,1,0:T(1,128)} %param.7) | copy-start | bytes 1540
  126.6 1.3 copy-start
Sparse Core Ops, SparseCore 0:
  8.9 23.9 all-gather.2
  35.0 41.4 all-gather.4
  128.1 30.9 reduce-scatter.1
where the time goes:
time: 169 us; the launch traced here: 168 us
  waiting for transfers between devices  78.3 us (46%)
  other arithmetic  32.1 us (19%)
  local copies, waits for them, and re-layouts  18 us (11%)
  matrix products  17.7 us (10%)
  between operations  13.2 us (8%)
  blocking collectives  8.72 us (5%)
    all_gather x1, waiting for transfers between devices, shards(): lax.all_gather(items, 'blk', axis=0, tiled=True)  35.9 us
    scatter-add x1, other arithmetic, accumulate(): return totals.at[user_ids].add(products)  24.4 us
    all_gather x1, waiting for transfers between devices, shards(): panel_rows = lax.all_gather(users, 'fiber', axis=1, tiled=True)  23.5 us
    reduce_scatter x1, waiting for transfers between devices, shards(): lax.psum_scatter(totals.reshape(-1, rank_width), 'fiber', scatter_dimensi...  17.5 us
    dot_general x1, matrix products, accumulate(): jnp.einsum('tab,tbr->tar', weight, item_rows, preferred_element_type=jnp....  17.4 us
    unnamed x1, blocking collectives  8.72 us
    gather x1, local copies, waits for them, and re-layouts, one_group(): gathered[item_ids]  8.15 us
    gather x1, local copies, waits for them, and re-layouts, accumulate(): user_rows = panel_blocks[user_ids]  7.74 us
  transfers between devices with their start and end apart: 3, of which 3 were waited for; matrix products, arithmetic and copies ran while one was open for 8% of the time, Pallas kernels for 0%

commit v1 on v0

--- a/solution.py
+++ b/solution.py
@@ -3,10 +3,15 @@
 import jax.numpy as jnp
 from jax import lax
 from jax.sharding import PartitionSpec as P
+from jax.lax import all_gather
 
 
 def shards(users, items, tile_users, tile_items, confidence):
-    panel_rows = lax.all_gather(users, "fiber", axis=1, tiled=True)
+
+    def trace_area(d0, in_array):
+        return jnp.concatenate(all_gather(in_array, "fiber"), d0)
+
+    panel_rows = trace_area(1, users)
     tile_size = confidence.shape[-1]
     rank_width = panel_rows.shape[1]
     user_count = panel_rows.shape[0] // tile_size

time: 169 us -> 168 us (level)
  transfers between devices with their start and end apart: 3 -> 3, of which waited for: 3 -> 3; matrix products, arithmetic and copies ran while one was open for 8% -> 9% of each run, Pallas kernels for 0% -> 0%
where the time goes in v1:
time: 168 us
  waiting for transfers between devices  77 us (46%)
  other arithmetic  32.1 us (19%)
  local copies, waits for them, and re-layouts  19.3 us (11%)
  matrix products  17.4 us (10%)
  between operations  13.2 us (8%)
  blocking collectives  8.71 us (5%)
    all_gather x1, waiting for transfers between devices, shards(): lax.all_gather(items, 'blk', axis=0, tiled=True)  34.6 us
    scatter-add x1, other arithmetic, accumulate(): return totals.at[user_ids].add(products)  24.4 us
    all_gather x1, waiting for transfers between devices, trace_area(): return jnp.concatenate(all_gather(in_array, 'fiber'), d0)  23.5 us
    reduce_scatter x1, waiting for transfers between devices, shards(): lax.psum_scatter(totals.reshape(-1, rank_width), 'fiber', scatter_dimensi...  17.5 us
    dot_general x1, matrix products, accumulate(): jnp.einsum('tab,tbr->tar', weight, item_rows, preferred_element_type=jnp....  17.1 us
    unnamed x1, blocking collectives  8.71 us
    gather x1, local copies, waits for them, and re-layouts, one_group(): gathered[item_ids]  8.16 us
    gather x1, local copies, waits for them, and re-layouts, accumulate(): user_rows = panel_blocks[user_ids]  6.53 us
  transfers between devices with their start and end apart: 3, of which 3 were waited for; matrix products, arithmetic and copies ran while one was open for 9% of the time, Pallas kernels for 0%

profile of v1, /device:TPU:0, one launch (start us, length us, event | category | flops | bytes accessed | tf_op | source)
XLA Modules:
  0.0 167.8 jit_solution(11953990467559425470)
XLA Ops:
  6.5 0.0 all-gather.6.cloned.1.call-start
  6.5 0.7 all-gather.6.cloned.1.call-update
  7.3 0.0 all-gather.4.cloned.1.call-start
  7.3 0.7 all-gather.4.cloned.1.call-update
  8.0 0.0 reduce-scatter.2.cloned.1.call-start
  8.1 0.7 fusion.9
  8.7 0.7 fusion.10
  9.4 23.5 %all-gather.6.cloned.1.call-done = bf16[4096,128]{1,0:T(8,128)(2,1)} async-done(((bf16[2048,128]{1,0:T(8,128)(2,1)}), bf16[4096,128]{1,0:T(8,128)(2,1)}) %all-gather.6.cloned.1.call-update) | async-done | bytes 1048592 | tf_op jit(solution)/shard_map/all_gather | solution.py:12
  32.9 1.5 copy.9
  34.4 0.2 copy.11
  34.6 0.8 copy.10
  35.4 6.5 %gather_fusion = bf16[128,128,256]{2,1,0:T(8,128)(2,1)} fusion(bf16[16,128,256]{2,1,0:T(8,128)(2,1)S(1)} %copy.10, s32[1024]{0:T(1024)S(1)} %pad_clamp_fusion.1), kind=kCustom, calls=%fused_computation | custom fusion | bytes 16777728 | tf_op jit(solution)/shard_map/while/body/eval_jaxpr/gather | solution.py:27
  42.0 34.6 %all-gather.4.cloned.1.call-done = bf16[4096,256]{1,0:T(8,128)(2,1)} async-done(((bf16[256,256]{1,0:T(8,128)(2,1)}), bf16[4096,256]{1,0:T(8,128)(2,1)}) %all-gather.4.cloned.1.call-update) | async-done | bytes 2097168 | tf_op jit(solution)/shard_map/all_gather | solution.py:38
  76.6 8.2 %gather_fusion.1 = bf16[128,128,256]{2,1,0:T(8,128)(2,1)} fusion(bf16[32,128,256]{2,1,0:T(8,128)(2,1)} %bitcast.34, s32[1024]{0:T(1024)S(1)} %pad_clamp_fusion), kind=kCustom, calls=%fused_computation.1 | custom fusion | bytes 16777728 | tf_op jit(solution)/shard_map/while/body/eval_jaxpr/gather | solution.py:49
  84.7 17.1 %fusion.2 = f32[128,128,256]{2,1,0:T(8,128)} fusion(bf16[128,128,256]{2,1,0:T(8,128)(2,1)} %gather_fusion.1, bf16[1,1,128,128,128]{4,3,2,1,0:T(8,128)(2,1)} %param.9, bf16[128,128,256]{2,1,0:T(8,128)(2,1)} %gather_fusion), kind=kOutput, calls=%fused_computation.7 | convolution fusion | flops 2155872256 | bytes 37748736 | tf_op jit(solution)/shard_map/while/body/eval_jaxpr/tab,tbr->tar/dot_general | solution.py:34
  101.8 0.2 broadcast_in_dim.16
  102.0 0.0 copy-start.2
  102.0 0.0 copy-start.1
  102.1 24.4 %scatter_fusion = f32[16,128,256]{2,1,0:T(8,128)S(1)} fusion(f32[16,128,256]{2,1,0:T(8,128)S(1)} %broadcast_in_dim.16, s32[128]{0:T(128)S(1)} %fusion.9, f32[128,128,256]{2,1,0:T(8,128)} %fusion.2), kind=kCustom, calls=%fused_computation.2 | custom fusion | flops 4194304 | bytes 50332160 | tf_op jit(solution)/shard_map/while/body/eval_jaxpr/scatter-add | solution.py:35
  126.4 0.0 copy-start
  126.4 1.3 copy-done
  127.8 0.0 reduce-scatter.2.cloned.1.call-update
  127.8 0.0 copy-done.2
  127.8 0.6 dynamic-slice
  128.4 3.4 %convert_reduce_fusion = f32[128,128]{1,0:T(8,128)S(1)} fusion(bf16[1,1,128,128,128]{4,3,2,1,0:T(8,128)(2,1)} %param.9), kind=kLoop, calls=%fused_computation.3 | loop fusion | flops 4177920 | bytes 4259840 | tf_op jit(solution)/shard_map/reduce_sum | solution.py:52
  131.8 0.0 copy-done.1
  131.8 0.3 convolution_bitcast_fusion
  132.1 8.7 %all-reduce = f32[2048,2]{0,1:T(2,128)S(1)} all-reduce(f32[2048,2]{0,1:T(2,128)S(1)} %broadcast_in_dim.18), channel_id=4, replica_groups=mesh['fiber'=2,'blk'=16] {'fiber'}, use_global_device_ids=true, to_apply=%region_3.0.clone | all-reduce | flops 4096 | bytes 32768
  140.8 0.7 fusion.8
  141.4 17.5 %reduce-scatter.2.cloned.1.call-done = f32[2048,128]{1,0:T(8,128)} async-done(((f32[2048,256]{1,0:T(8,128)}), f32[2048,128]{1,0:T(8,128)}) %reduce-scatter.2.cloned.1.call-update) | async-done | bytes 1048592 | tf_op jit(solution)/shard_map/reduce_scatter | solution.py:60
  158.9 2.4 %multiply_convert_fusion = bf16[2048,128]{1,0:T(8,128)(2,1)} fusion(f32[2048,128]{1,0:T(8,128)} %reduce-scatter.2.cloned.1.call-done, f32[2048]{0:T(1024)S(1)} %bitcast.38), kind=kLoop, calls=%fused_computation.11 | loop fusion | flops 524288 | bytes 1581056 | tf_op jit(solution)/shard_map/convert_element_type | solution.py:63
  (3 shorter events, 0.0 us)
Async XLA Ops:
  6.5 26.4 %all-gather.6.cloned.1.call-start = ((), (), s32[]{:S(2)}) async-start(), calls=%async_computation.3 | async-start | bytes 1572864 | tf_op jit(solution)/shard_map/all_gather | solution.py:12
  7.3 69.3 %all-gather.4.cloned.1.call-start = ((), (), s32[]{:S(2)}) async-start(), calls=%async_computation.1 | async-start | bytes 2228224 | tf_op jit(solution)/shard_map/all_gather | solution.py:38
  8.0 150.9 %reduce-scatter.2.cloned.1.call-start = ((), (), s32[]{:S(2)}) async-start(), calls=%async_computation.2 | async-start | bytes 3145728 | tf_op jit(solution)/shard_map/reduce_scatter | solution.py:60
  102.0 25.8 %copy-start.2 = (u32[32]{0:T(128)S(1)}, u32[32]{0:T(128)}, u32[]{:S(2)}) copy-start(u32[32]{0:T(128)} %constant.29) | copy-start | bytes 388
  102.0 29.7 %copy-start.1 = (s32[1,1,128]{2,1,0:T(1,128)S(1)}, s32[1,1,128]{2,1,0:T(1,128)}, u32[]{:S(2)}) copy-start(s32[1,1,128]{2,1,0:T(1,128)} %param.7) | copy-start | bytes 1540
  126.4 1.3 copy-start
Sparse Core Ops, SparseCore 0:
  8.9 23.9 all-gather.5
  35.1 41.4 all-gather.3
  127.9 30.9 reduce-scatter.1
